TPU v7x, 32 devices: a whole 2x2x4 slice. The times are simulated.
32 devices in a mesh: groups: 2 (over y), patch: 8 (over z, x), req: 2 (over core).
Axes of the slice: x: 2, y: 2, z: 4, core: 2. Of those that a mesh axis runs over, the one named last changes fastest.
Arguments:
- hidden: float32 [16, 8, 64, 1280], P(('groups', 'req'), 'patch'), parts along dimension 0
- skip: float32 [16, 8, 64, 1280], P(('groups', 'req'), 'patch'), parts along dimension 0, may hold values from -6 to 6
- timestep_embedding_table: float32 [50, 1280], replicated, may hold values from -5 to 5
- timesteps: int32 [16], P(('groups', 'req')), parts along dimension 0, may hold values from 0 to 49, as said below
- group_norm_gain: float32 [1280], replicated, may hold values from 0.1 to 1.9
- group_norm_bias: float32 [1280], replicated, may hold values from -3 to 3
- kernel_weight: bfloat16 [9, 1280, 1280], P(None, 'patch', 'req'), may hold values from -0.0546875 to 0.0546875
- adapter_down_weight: bfloat16 [32, 64, 11520], P(('groups', 'patch')), parts along dimension 0, may hold values from -0.0546875 to 0.0546875
- adapter_up_weight: bfloat16 [32, 64, 1280], P(('groups', 'patch')), parts along dimension 0, may hold values from -0.75 to 0.75
- request_adapter: int32 [16], P(('groups', 'req')), parts along dimension 0, may hold values from 0 to 15
- adapter_row_table: int32 [32], P('groups'), parts along dimension 0, may hold values from 0 to 15, each once
Outputs:
- block_out: float32 [16, 8, 64, 1280], P(('groups', 'req'), 'patch'), parts along dimension 0
There are 2 independent parts, one for each index of `groups`. A program takes and returns all parts, laid end to end along the dimension named above; an argument that names none is the same for every part. Nothing has to cross between parts.
Inputs may be any that keep to these rules, and one draw needn't show every extreme that they name: adapter_row_table[a] is the store row of adapter a; every row is used once. Requests 0 and 1 have different timesteps.
All inputs are finite; a program needn't handle non-finite values.
Results may differ from a plain program's by a relative error of at most 0.0026.
Values may be sent and summed in bfloat16 or wider, within the bound.
A program may use at most 128 MiB of HBM per device.

v0:
```python
import jax
import jax.numpy as jnp
from jax import lax
from jax.sharding import PartitionSpec as P

GROUPS = 32


def broadcast(block, axis, owner):
    block = jnp.where(lax.axis_index(axis) == owner, block, jnp.zeros_like(block))
    return lax.psum(block, axis)


def padded(cells, sides, width):
    for axis, dim in sides:
        count = lax.axis_size(axis)
        ends = count - 1
        head = lax.slice_in_dim(cells, 0, width, axis=dim)
        tail = lax.slice_in_dim(cells, cells.shape[dim] - width, cells.shape[dim], axis=dim)
        cells = jnp.concatenate(
            [
                lax.ppermute(tail, axis, [(i, (i + 1) % count) for i in range(ends)]),
                cells,
                lax.ppermute(head, axis, [((i + 1) % count, i) for i in range(ends)]),
            ],
            axis=dim,
        )
    return cells


def from_partner(x, axis, stride):
    return lax.ppermute(x, axis, [(i, i ^ 1 << stride) for i in range(lax.axis_size(axis))])


def make_taps(extended, rows, width):
    pieces = [extended[:, dy : dy + rows, dx : dx + width, :] for dy in range(3) for dx in range(3)]
    stacked = jnp.stack(pieces, axis=3)
    count = stacked.shape[0] * rows * width
    return stacked.reshape(count, 9, stacked.shape[-1])


def load_adapter_factors(
    adapter_down_weight, adapter_up_weight, request_adapter, adapter_row_table, request_total
):
    resident_count = adapter_down_weight.shape[0]
    fetched = []
    for request in range(request_total):
        resident_row = adapter_row_table[request_adapter[request]]
        owner = resident_row // resident_count
        store_position = resident_row % resident_count
        resident_down = lax.dynamic_index_in_dim(
            adapter_down_weight, store_position, 0, keepdims=False
        )
        resident_up = lax.dynamic_index_in_dim(adapter_up_weight, store_position, 0, keepdims=False)
        fetched.append(
            (broadcast(resident_down, "patch", owner), broadcast(resident_up, "patch", owner))
        )
    return fetched


def shards(
    hidden,
    skip,
    timestep_embedding_table,
    timesteps,
    group_norm_gain,
    group_norm_bias,
    kernel_weight,
    adapter_down_weight,
    adapter_up_weight,
    request_adapter,
    adapter_row_table,
):
    request_total, rows, width, chans = hidden.shape
    steps_count = timestep_embedding_table.shape[0]
    onehot = (timesteps[:, None] == jnp.arange(steps_count, dtype=jnp.int32)[None, :]).astype(
        jnp.float32
    )
    temb = jnp.dot(
        onehot,
        timestep_embedding_table,
        preferred_element_type=jnp.float32,
        precision=lax.Precision.HIGHEST,
    )
    shifted = hidden + temb[:, None, None, :]
    grouped = shifted.reshape(request_total, rows, width, GROUPS, chans // GROUPS)
    count = rows * lax.axis_size("patch") * width * (chans // GROUPS)
    totals = lax.psum(jnp.sum(grouped, axis=(1, 2, 4)), "patch")
    mean = totals / count
    centered = grouped - mean[:, None, None, :, None]
    squares = lax.psum(jnp.sum(centered * centered, axis=(1, 2, 4)), "patch")
    var = squares / count
    normed = (centered * lax.rsqrt(var + 1e-05)[:, None, None, :, None]).reshape(
        request_total, rows, width, chans
    )
    act = jax.nn.silu(normed * group_norm_gain + group_norm_bias).astype(jnp.bfloat16)
    extended = padded(act, (("patch", 1),), 1)
    extended = jnp.pad(extended, ((0, 0), (0, 0), (1, 1), (0, 0)))
    partner = from_partner(extended, "req", 0)
    taps = make_taps(jnp.concatenate([extended, partner], axis=0), rows, width)
    pixels = request_total * rows * width
    conv_half = jnp.einsum(
        "ptc,tco->po",
        taps,
        lax.all_gather(kernel_weight, "patch", axis=1, tiled=True),
        preferred_element_type=jnp.float32,
    )
    own_half = conv_half[:pixels]
    returned = from_partner(conv_half[pixels:], "req", 0)
    first = lax.axis_index("req") == 0
    left_half = jnp.where(first, own_half, returned)
    right_half = jnp.where(first, returned, own_half)
    conv = jnp.concatenate([left_half, right_half], axis=1).reshape(
        request_total, rows * width, chans
    )
    own_taps = taps[:pixels].reshape(request_total, rows * width, 9 * chans)
    adapter_factors = load_adapter_factors(
        adapter_down_weight, adapter_up_weight, request_adapter, adapter_row_table, request_total
    )
    deltas = []
    for request in range(request_total):
        down_factor, upper_limit = adapter_factors[request]
        low = lax.dot_general(
            own_taps[request],
            down_factor,
            (((1,), (1,)), ((), ())),
            preferred_element_type=jnp.float32,
        ).astype(jnp.bfloat16)
        deltas.append(jnp.dot(low, upper_limit, preferred_element_type=jnp.float32))
    total = conv + jnp.stack(deltas, axis=0)
    return skip + total.reshape(request_total, rows, width, chans)


def solution(mesh):
    return jax.shard_map(
        shards,
        mesh=mesh,
        in_specs=(
            P(("groups", "req"), "patch", None, None),
            P(("groups", "req"), "patch", None, None),
            P(),
            P(("groups", "req")),
            P(),
            P(),
            P(None, "patch", "req"),
            P(("groups", "patch"), None, None),
            P(("groups", "patch"), None, None),
            P(("groups", "req")),
            P("groups"),
        ),
        out_specs=P(("groups", "req"), "patch", None, None),
        check_vma=False,
    )
```

profile of v0, /device:TPU:1, one launch (start us, length us, event | category | flops | bytes accessed | tf_op | source)
XLA Modules:
  0.0 518.1 jit_solution(13756354301383934993)
XLA Ops:
  6.5 1.5 fusion.27
  15.8 1.5 fusion.26
  27.7 5.8 %select_bitcast_fusion.3 = (bf16[64,11520]{1,0:T(8,128)(2,1)}, bf16[64,11520]{1,0:T(8,128)(2,1)}, bf16[64,11520]{1,0:T(8,128)(2,1)}, bf16[64,11520]{1,0:T(8,128)(2,1)}) fusion(bf16[2,64,11520]{2,1,0:T(8,128)(2,1)} %param.18, s32[]{:T(128)S(6)} %select_n.157, pred[]{:T(512)S(6)} %eq.41, s32[]{:T(128)S(6)} %select_n.167, pred[]{:T(512)S(6)} %eq.42, ...), kind=kLoop, calls=%fused_computation.31 | loop fusion | flops 2949120 | bytes 11796500 | tf_op jit(solution)/shard_map/jit(_where)/select_n | solution.py:10
  36.0 19.5 %psum.70 = f32[4,32]{1,0:T(4,128)S(1)} all-reduce(f32[4,32]{1,0:T(4,128)S(1)} %reduce_sum.25), channel_id=1, replica_groups=mesh['groups'=2,'patch'=8,'req'=2] {'patch'}, use_global_device_ids=true, to_apply=%region_2.0 | all-reduce | flops 128 | bytes 1024 | tf_op jit(solution)/shard_map/psum | solution.py:88
  56.2 15.0 %psum.71 = f32[4,32]{1,0:T(4,128)S(1)} all-reduce(f32[4,32]{1,0:T(4,128)S(1)} %reduce_sum.37), channel_id=1, replica_groups=mesh['groups'=2,'patch'=8,'req'=2] {'patch'}, use_global_device_ids=true, to_apply=%region_5.6 | all-reduce | flops 128 | bytes 1024 | tf_op jit(solution)/shard_map/psum | solution.py:91
  71.9 3.5 collective-permute-start
  75.3 1.5 collective-permute-start.1
  76.8 28.0 %collective-permute-done = bf16[4,1,64,1280]{3,2,1,0:T(8,128)(2,1)S(1)} collective-permute-done((bf16[4,1,64,1280]{3,2,1,0:T(8,128)(2,1)S(1)}, bf16[4,1,64,1280]{3,2,1,0:T(8,128)(2,1)S(1)}, u32[]{:S(2)}, u32[]{:S(2)}) %collective-permute-start) | collective-permute-done | bytes 655392 | tf_op jit(solution)/shard_map/ppermute | solution.py:22
  105.6 4.5 collective-permute-start.2
  110.1 4.1 collective-permute-done.2
  115.4 1.5 bitcast_dynamic-update-slice_fusion.6
  116.9 1.5 bitcast_dynamic-update-slice_fusion.5
  119.7 1.5 bitcast_dynamic-update-slice_fusion.3
  121.2 1.5 bitcast_dynamic-update-slice_fusion.2
  123.9 1.5 bitcast_dynamic-update-slice_fusion
  126.9 4.3 copy-done.3
  131.2 3.1 fusion.25
  147.5 128.3 %all-reduce.4.cloned.1.call-done = (bf16[64,1280]{1,0:T(8,128)(2,1)}, bf16[64,11520]{1,0:T(8,128)(2,1)}, bf16[64,1280]{1,0:T(8,128)(2,1)}, bf16[64,11520]{1,0:T(...) async-done(((bf16[64,1280]{1,0:T(8,128)(2,1)}, bf16[64,11520]{1,0:T(8,128)(2,1)}, ...) | async-done | bytes 6553616 | tf_op jit(solution)/shard_map/psum | solution.py:11
  275.8 3.3 convolution_bitcast_fusion.3
  279.1 200.0 %all-gather.2.cloned.1.call-done = bf16[9,1280,640]{2,1,0:T(8,128)(2,1)} async-done(((bf16[9,160,640]{2,1,0:T(8,128)(2,1)}), bf16[9,1280,640]{2,1,0:T(8,128)(2,1)}) %all-gather.2.cloned.1.call-update) | async-done | bytes 14745616 | tf_op jit(solution)/shard_map/all_gather | solution.py:105
  479.1 16.5 %convolution_bitcast_fusion.4 = f32[512,640]{1,0:T(8,128)S(1)} fusion(bf16[512,9,1280]{2,0,1:T(8,128)(2,1)} %constant_dynamic-update-slice_fusion, bf16[9,1280,640]{2,1,0:T(8,128)(2,1)} %all-gather.2.cloned.1.call-done), kind=kOutput, calls=%fused_computation.32 | convolution fusion | flops 7549747200 | bytes 27852800 | tf_op jit(solution)/shard_map/ptc,tco->po/dot_general | solution.py:102
  498.7 3.3 convolution_bitcast_fusion.2
  502.0 2.9 convolution_bitcast_fusion.1
  504.9 2.2 convolution_bitcast_fusion
  (77 shorter events, 30.0 us)
Async XLA Ops:
  6.5 28.6 %copy-start = (f32[50,1280]{1,0:T(8,128)S(1)}, f32[50,1280]{1,0:T(8,128)}, u32[]{:S(2)}) copy-start(f32[50,1280]{1,0:T(8,128)} %param.13) | copy-start | bytes 768004
  6.5 269.2 %all-reduce.4.cloned.1.call-start = ((), (), s32[]{:S(2)}) async-start(), calls=%async_computation.1 | async-start | bytes 13107200 | tf_op jit(solution)/shard_map/psum | solution.py:11
  27.7 5.8 %copy-start.8 = (bf16[2,64,1280]{2,1,0:T(8,128)(2,1)S(1)}, bf16[2,64,1280]{2,1,0:T(8,128)(2,1)}, u32[]{:S(2)}) copy-start(bf16[2,64,1280]{2,1,0:T(8,128)(2,1)} %param.19) | copy-start | bytes 983044
  34.4 0.8 copy-start.16
  34.4 1.3 copy-start.2
  34.4 444.7 %all-gather.2.cloned.1.call-start = ((), (), s32[]{:S(2)}) async-start(), calls=%async_computation | async-start | bytes 16588800 | tf_op jit(solution)/shard_map/all_gather | solution.py:105
  35.7 35.7 %copy-start.14 = (f32[1280]{0:T(1024)S(1)}, f32[1280]{0:T(1024)}, u32[]{:S(2)}) copy-start(f32[1280]{0:T(1024)} %param.16) | copy-start | bytes 15364
  35.7 35.7 %copy-start.15 = (f32[1280]{0:T(1024)S(1)}, f32[1280]{0:T(1024)}, u32[]{:S(2)}) copy-start(f32[1280]{0:T(1024)} %param.15) | copy-start | bytes 15364
  71.9 33.0 %collective-permute-start = (bf16[4,1,64,1280]{3,2,1,0:T(8,128)(2,1)S(1)}, bf16[4,1,64,1280]{3,2,1,0:T(8,128)(2,1)S(1)}, u32[]{:S(2)}, u32[]{:S(2)}) collective-permute-start(bf16[4,1,64,1280]{3,2,1,0:T(8,128)(2,1)S(1)} %multiply_convert_fusion), channel_id=1, source_target_pairs={{0,2},{2,4},{4,6},{6,8},{8,10},{10,12},{12,14},{1,3},{3,5},{5,7},{... | collective-permute-start | bytes 1966088 | tf_op jit(solution)/shard_map/ppermute | solution.py:22
  75.3 29.5 %collective-permute-start.1 = (bf16[4,1,64,1280]{3,2,1,0:T(8,128)(2,1)S(1)}, bf16[4,1,64,1280]{3,2,1,0:T(8,128)(2,1)S(1)}, u32[]{:S(2)}, u32[]{:S(2)}) collective-permute-start(bf16[4,1,64,1280]{3,2,1,0:T(8,128)(2,1)S(1)} %multiply_convert_fusion), channel_id=1, source_target_pairs={{2,0},{4,2},{6,4},{8,6},{10,8},{12,10},{14,12},{3,1},{5,3},{7,5},{... | collective-permute-start | bytes 1966088 | tf_op jit(solution)/shard_map/ppermute | solution.py:24
  105.6 8.5 %collective-permute-start.2 = (bf16[4,3,66,1280]{3,2,1,0:T(8,128)(2,1)S(1)}, bf16[4,3,66,1280]{3,2,1,0:T(8,128)(2,1)}, u32[]{:S(2)}, u32[]{:S(2)}) collective-permute-start(bf16[4,3,66,1280]{3,2,1,0:T(8,128)(2,1)S(1)} %fusion.5), channel_id=1, source_target_pairs={{0,1},{1,0},{2,3},{3,2},{4,5},{5,4},{6,7},{7,6},{8,9},{9,8},{10,11... | collective-permute-start | bytes 6082568 | tf_op jit(solution)/shard_map/ppermute | solution.py:32
  126.9 4.3 copy-start.3
  279.1 219.6 %copy-start.13 = (bf16[64,1280]{1,0:T(8,128)(2,1)S(1)}, bf16[64,1280]{1,0:T(8,128)(2,1)}, u32[]{:S(2)}) copy-start(bf16[64,1280]{1,0:T(8,128)(2,1)} %get-tuple-element.9) | copy-start | bytes 491524
  495.6 1.1 copy-start.9
  497.6 9.6 %collective-permute-start.3 = (f32[256,640]{1,0:T(8,128)}, f32[256,640]{1,0:T(8,128)}, u32[]{:S(2)}, u32[]{:S(2)}) collective-permute-start(f32[256,640]{1,0:T(8,128)} %slice.103), channel_id=1, source_target_pairs={{0,1},{1,0},{2,3},{3,2},{4,5},{5,4},{6,7},{7,6},{8,9},{9,8},{10,11... | collective-permute-start | bytes 1966088 | tf_op jit(solution)/shard_map/ppermute | solution.py:32
  498.7 3.3 copy-start.12
  502.0 2.9 copy-start.11
  504.9 2.3 copy-start.10
  508.4 1.3 copy-start.4
  508.4 1.4 copy-start.5
  508.4 1.4 copy-start.6
  508.4 1.5 copy-start.7
  508.5 2.7 copy-start.1
Sparse Core Ops, SparseCore 0:
  34.5 241.2 all-reduce.3
  278.0 201.0 all-gather.1
where the time goes:
time: 519 us; the launch traced here: 518 us
  waiting for transfers between devices  361 us (70%)
  blocking collectives  34.5 us (7%)
  between operations  31.9 us (6%)
  matrix products  28.6 us (6%)
  local copies, waits for them, and re-layouts  27.8 us (5%)
  other arithmetic  23.6 us (5%)
  starting transfers between devices  10.5 us (2%)
    all_gather x1, waiting for transfers between devices, shards(): lax.all_gather(kernel_weight, 'patch', axis=1, tiled=True)  200 us
    psum x1, waiting for transfers between devices, broadcast(): return lax.psum(block, axis)  128 us
    ppermute x1, waiting for transfers between devices, padded(): lax.ppermute(tail, axis, [(i, (i + 1) % count) for i in range(ends)])  28 us
    psum x1, blocking collectives, shards(): totals = lax.psum(jnp.sum(grouped, axis=(1, 2, 4)), 'patch')  19.5 us
    unnamed x46, local copies, waits for them, and re-layouts  19.1 us
    dot_general x1, matrix products, shards(): jnp.einsum('ptc,tco->po', taps, lax.all_gather(kernel_weight, 'patch', ax...  16.5 us
    psum x1, blocking collectives, shards(): squares = lax.psum(jnp.sum(centered * centered, axis=(1, 2, 4)), 'patch')  15 us
    dot_general x4, matrix products, shards(): deltas.append(jnp.dot(low, upper_limit, preferred_element_type=jnp.float32))  11.8 us
  transfers between devices with their start and end apart: 6, of which 4 were waited for; matrix products, arithmetic and copies ran while one was open for 8% of the time, Pallas kernels for 0%

commit v1 on v0

--- a/solution.py
+++ b/solution.py
@@ -88,7 +88,7 @@
     totals = lax.psum(jnp.sum(grouped, axis=(1, 2, 4)), "patch")
     mean = totals / count
     centered = grouped - mean[:, None, None, :, None]
-    squares = lax.psum(jnp.sum(centered * centered, axis=(1, 2, 4)), "patch")
+    squares = jnp.sum(lax.all_gather(jnp.sum(centered * centered, axis=(1, 2, 4)), "patch"), axis=0)
     var = squares / count
     normed = (centered * lax.rsqrt(var + 1e-05)[:, None, None, :, None]).reshape(
         request_total, rows, width, chans

time: 519 us -> 519 us (level)
  blocking collectives: 34.5 us -> 43.8 us
  waiting for transfers between devices: 361 us -> 352 us
    all_gather x0 -> x1, blocking collectives: none -> 24.3 us  [shards(): lax.all_gather(jnp.sum(centered * centered, axis=(1, 2, 4)), 'patch')]
    psum x1 -> x0, blocking collectives: 15 us -> none  [shards(): squares = lax.psum(jnp.sum(centered * centered, axis=(1, 2, 4)), 'patch')]
    ppermute x1, waiting for transfers between devices: 28 us -> 14.9 us  [padded(): lax.ppermute(tail, axis, [(i, (i + 1) % count) for i in range(ends)])]
where the time goes in v1:
time: 519 us; the launch traced here: 518 us
  waiting for transfers between devices  352 us (68%)
  blocking collectives  43.8 us (8%)
  between operations  31.9 us (6%)
  matrix products  28.6 us (6%)
  local copies, waits for them, and re-layouts  27.8 us (5%)
  other arithmetic  23.7 us (5%)
  starting transfers between devices  9.93 us (2%)
    all_gather x1, waiting for transfers between devices, shards(): lax.all_gather(kernel_weight, 'patch', axis=1, tiled=True)  200 us
    psum x1, waiting for transfers between devices, broadcast(): return lax.psum(block, axis)  132 us
    all_gather x1, blocking collectives, shards(): lax.all_gather(jnp.sum(centered * centered, axis=(1, 2, 4)), 'patch')  24.3 us
    psum x1, blocking collectives, shards(): totals = lax.psum(jnp.sum(grouped, axis=(1, 2, 4)), 'patch')  19.5 us
    unnamed x46, local copies, waits for them, and re-layouts  19.1 us
    dot_general x1, matrix products, shards(): jnp.einsum('ptc,tco->po', taps, lax.all_gather(kernel_weight, 'patch', ax...  16.5 us
    ppermute x1, waiting for transfers between devices, padded(): lax.ppermute(tail, axis, [(i, (i + 1) % count) for i in range(ends)])  14.9 us
    dot_general x4, matrix products, shards(): deltas.append(jnp.dot(low, upper_limit, preferred_element_type=jnp.float32))  11.8 us
  transfers between devices with their start and end apart: 6, of which 4 were waited for; matrix products, arithmetic and copies ran while one was open for 8% of the time, Pallas kernels for 0%

profile of v1, /device:TPU:1, one launch (start us, length us, event | category | flops | bytes accessed | tf_op | source)
XLA Modules:
  0.0 517.6 jit_solution(8946679550984637128)
XLA Ops:
  6.5 1.5 fusion.27
  15.8 1.5 fusion.26
  27.7 5.8 %select_bitcast_fusion.3 = (bf16[64,11520]{1,0:T(8,128)(2,1)}, bf16[64,11520]{1,0:T(8,128)(2,1)}, bf16[64,11520]{1,0:T(8,128)(2,1)}, bf16[64,11520]{1,0:T(8,128)(2,1)}) fusion(bf16[2,64,11520]{2,1,0:T(8,128)(2,1)} %param.18, s32[]{:T(128)S(6)} %select_n.157, pred[]{:T(512)S(6)} %eq.41, s32[]{:T(128)S(6)} %select_n.167, pred[]{:T(512)S(6)} %eq.42, ...), kind=kLoop, calls=%fused_computation.31 | loop fusion | flops 2949120 | bytes 11796500 | tf_op jit(solution)/shard_map/jit(_where)/select_n | solution.py:10
  36.0 19.5 %psum.63 = f32[4,32]{1,0:T(4,128)S(1)} all-reduce(f32[4,32]{1,0:T(4,128)S(1)} %reduce_sum.36), channel_id=1, replica_groups=mesh['groups'=2,'patch'=8,'req'=2] {'patch'}, use_global_device_ids=true, to_apply=%region_2.0 | all-reduce | flops 128 | bytes 1024 | tf_op jit(solution)/shard_map/psum | solution.py:88
  56.2 24.3 %all-gather.1 = f32[8,4,32]{2,1,0:T(4,128)S(1)} all-gather(f32[1,4,32]{2,1,0:T(4,128)S(1)} %bitcast.138), channel_id=2, replica_groups=mesh['groups'=2,'patch'=8,'req'=2] {'patch'}, dimensions={0}, use_global_device_ids=true | all-gather | bytes 4608 | tf_op jit(solution)/shard_map/all_gather | solution.py:91
  82.5 1.5 collective-permute-start.1
  84.0 14.9 %collective-permute-done = bf16[4,1,64,1280]{3,2,1,0:T(8,128)(2,1)S(1)} collective-permute-done((bf16[4,1,64,1280]{3,2,1,0:T(8,128)(2,1)S(1)}, bf16[4,1,64,1280]{3,2,1,0:T(8,128)(2,1)S(1)}, u32[]{:S(2)}, u32[]{:S(2)}) %collective-permute-start) | collective-permute-done | bytes 655392 | tf_op jit(solution)/shard_map/ppermute | solution.py:22
  99.7 6.0 %collective-permute-start.2 = (bf16[4,3,66,1280]{3,2,1,0:T(8,128)(2,1)S(1)}, bf16[4,3,66,1280]{3,2,1,0:T(8,128)(2,1)}, u32[]{:S(2)}, u32[]{:S(2)}) collective-permute-start(bf16[4,3,66,1280]{3,2,1,0:T(8,128)(2,1)S(1)} %fusion.5), channel_id=1, source_target_pairs={{0,1},{1,0},{2,3},{3,2},{4,5},{5,4},{6,7},{7,6},{8,9},{9,8},{10,11... | collective-permute-start | bytes 6082568 | tf_op jit(solution)/shard_map/ppermute | solution.py:32
  105.7 4.1 collective-permute-done.2
  111.0 1.5 bitcast_dynamic-update-slice_fusion.6
  112.5 1.5 bitcast_dynamic-update-slice_fusion.5
  115.3 1.5 bitcast_dynamic-update-slice_fusion.3
  116.8 1.5 bitcast_dynamic-update-slice_fusion.2
  119.5 1.5 bitcast_dynamic-update-slice_fusion
  121.0 1.5 bitcast_dynamic-update-slice_fusion.8
  122.5 4.3 copy-done.3
  126.8 3.1 fusion.25
  143.1 132.2 %all-reduce.4.cloned.1.call-done = (bf16[64,1280]{1,0:T(8,128)(2,1)}, bf16[64,11520]{1,0:T(8,128)(2,1)}, bf16[64,1280]{1,0:T(8,128)(2,1)}, bf16[64,11520]{1,0:T(...) async-done(((bf16[64,1280]{1,0:T(8,128)(2,1)}, bf16[64,11520]{1,0:T(8,128)(2,1)}, ...) | async-done | bytes 6553616 | tf_op jit(solution)/shard_map/psum | solution.py:11
  275.3 3.3 convolution_bitcast_fusion.3
  278.6 200.0 %all-gather.4.cloned.1.call-done = bf16[9,1280,640]{2,1,0:T(8,128)(2,1)} async-done(((bf16[9,160,640]{2,1,0:T(8,128)(2,1)}), bf16[9,1280,640]{2,1,0:T(8,128)(2,1)}) %all-gather.4.cloned.1.call-update) | async-done | bytes 14745616 | tf_op jit(solution)/shard_map/all_gather | solution.py:105
  478.6 16.5 %convolution_bitcast_fusion.4 = f32[512,640]{1,0:T(8,128)S(1)} fusion(bf16[512,9,1280]{2,0,1:T(8,128)(2,1)} %constant_dynamic-update-slice_fusion, bf16[9,1280,640]{2,1,0:T(8,128)(2,1)} %all-gather.4.cloned.1.call-done), kind=kOutput, calls=%fused_computation.32 | convolution fusion | flops 7549747200 | bytes 27852800 | tf_op jit(solution)/shard_map/ptc,tco->po/dot_general | solution.py:102
  498.2 3.3 convolution_bitcast_fusion.2
  501.6 2.9 convolution_bitcast_fusion.1
  504.5 2.2 convolution_bitcast_fusion
  (78 shorter events, 29.9 us)
Async XLA Ops:
  6.5 28.6 %copy-start = (f32[50,1280]{1,0:T(8,128)S(1)}, f32[50,1280]{1,0:T(8,128)}, u32[]{:S(2)}) copy-start(f32[50,1280]{1,0:T(8,128)} %param.13) | copy-start | bytes 768004
  6.5 268.8 %all-reduce.4.cloned.1.call-start = ((), (), s32[]{:S(2)}) async-start(), calls=%async_computation.1 | async-start | bytes 13107200 | tf_op jit(solution)/shard_map/psum | solution.py:11
  27.7 5.8 %copy-start.8 = (bf16[2,64,1280]{2,1,0:T(8,128)(2,1)S(1)}, bf16[2,64,1280]{2,1,0:T(8,128)(2,1)}, u32[]{:S(2)}) copy-start(bf16[2,64,1280]{2,1,0:T(8,128)(2,1)} %param.19) | copy-start | bytes 983044
  34.4 0.8 copy-start.16
  34.4 1.3 copy-start.2
  34.4 444.2 %all-gather.4.cloned.1.call-start = ((), (), s32[]{:S(2)}) async-start(), calls=%async_computation | async-start | bytes 16588800 | tf_op jit(solution)/shard_map/all_gather | solution.py:105
  35.7 45.0 %copy-start.14 = (f32[1280]{0:T(1024)S(1)}, f32[1280]{0:T(1024)}, u32[]{:S(2)}) copy-start(f32[1280]{0:T(1024)} %param.16) | copy-start | bytes 15364
  35.7 45.0 %copy-start.15 = (f32[1280]{0:T(1024)S(1)}, f32[1280]{0:T(1024)}, u32[]{:S(2)}) copy-start(f32[1280]{0:T(1024)} %param.15) | copy-start | bytes 15364
  81.2 17.7 %collective-permute-start = (bf16[4,1,64,1280]{3,2,1,0:T(8,128)(2,1)S(1)}, bf16[4,1,64,1280]{3,2,1,0:T(8,128)(2,1)S(1)}, u32[]{:S(2)}, u32[]{:S(2)}) collective-permute-start(bf16[4,1,64,1280]{3,2,1,0:T(8,128)(2,1)S(1)} %multiply_convert_fusion), channel_id=1, source_target_pairs={{0,2},{2,4},{4,6},{6,8},{8,10},{10,12},{12,14},{1,3},{3,5},{5,7},{... | collective-permute-start | bytes 1966088 | tf_op jit(solution)/shard_map/ppermute | solution.py:22
  82.5 16.4 %collective-permute-start.1 = (bf16[4,1,64,1280]{3,2,1,0:T(8,128)(2,1)S(1)}, bf16[4,1,64,1280]{3,2,1,0:T(8,128)(2,1)S(1)}, u32[]{:S(2)}, u32[]{:S(2)}) collective-permute-start(bf16[4,1,64,1280]{3,2,1,0:T(8,128)(2,1)S(1)} %multiply_convert_fusion), channel_id=1, source_target_pairs={{2,0},{4,2},{6,4},{8,6},{10,8},{12,10},{14,12},{3,1},{5,3},{7,5},{... | collective-permute-start | bytes 1966088 | tf_op jit(solution)/shard_map/ppermute | solution.py:24
  99.7 10.1 %collective-permute-start.2 = (bf16[4,3,66,1280]{3,2,1,0:T(8,128)(2,1)S(1)}, bf16[4,3,66,1280]{3,2,1,0:T(8,128)(2,1)}, u32[]{:S(2)}, u32[]{:S(2)}) collective-permute-start(bf16[4,3,66,1280]{3,2,1,0:T(8,128)(2,1)S(1)} %fusion.5), channel_id=1, source_target_pairs={{0,1},{1,0},{2,3},{3,2},{4,5},{5,4},{6,7},{7,6},{8,9},{9,8},{10,11... | collective-permute-start | bytes 6082568 | tf_op jit(solution)/shard_map/ppermute | solution.py:32
  122.5 4.3 copy-start.3
  278.6 219.6 %copy-start.13 = (bf16[64,1280]{1,0:T(8,128)(2,1)S(1)}, bf16[64,1280]{1,0:T(8,128)(2,1)}, u32[]{:S(2)}) copy-start(bf16[64,1280]{1,0:T(8,128)(2,1)} %get-tuple-element.9) | copy-start | bytes 491524
  495.2 1.1 copy-start.9
  497.1 9.6 %collective-permute-start.3 = (f32[256,640]{1,0:T(8,128)}, f32[256,640]{1,0:T(8,128)}, u32[]{:S(2)}, u32[]{:S(2)}) collective-permute-start(f32[256,640]{1,0:T(8,128)} %slice.103), channel_id=1, source_target_pairs={{0,1},{1,0},{2,3},{3,2},{4,5},{5,4},{6,7},{7,6},{8,9},{9,8},{10,11... | collective-permute-start | bytes 1966088 | tf_op jit(solution)/shard_map/ppermute | solution.py:32
  498.2 3.3 copy-start.12
  501.6 2.9 copy-start.11
  504.5 2.2 copy-start.10
  507.9 1.3 copy-start.4
  507.9 1.4 copy-start.5
  508.0 1.4 copy-start.6
  508.0 1.5 copy-start.7
  508.1 2.7 copy-start.1
Sparse Core Ops, SparseCore 0:
  34.5 240.8 all-reduce.3
  277.5 201.0 all-gather.3
